TPU v7x, 128 devices: a whole 4x4x4 slice. The times are simulated.
128 devices in a mesh: leaf: 32 (over x, y, core), chain: 4 (over z).
Axes of the slice: x: 4, y: 4, z: 4, core: 2. Of those that a mesh axis runs over, the one named last changes fastest.
Arguments:
- right_side: float32 [32, 4096, 1024], P('leaf', 'chain'), may hold values from -6 to 6
- lower_rows: bfloat16 [32, 4096, 4096], P('leaf', 'chain'), may hold values from -0.09375 to 0.09375
- block_inverse: bfloat16 [32, 4096, 1024], P('leaf', 'chain'), may hold values from -0.1875 to 0.1875
- ancestor_cols: bfloat16 [32, 3072, 4096], P('leaf', None, 'chain'), may hold values from -0.09375 to 0.09375
- pattern: int32 [32, 24], P('leaf'), may hold values 0 or 1
- ancestor_side: float32 [3072, 1024], P('chain'), may hold values from -24 to 24
- ancestor_inverse: bfloat16 [3072, 768], P('chain'), may hold values from -0.21875 to 0.21875
Outputs:
- solution: float32 [32, 4096, 1024], P('leaf', 'chain')
- ancestor_solution: float32 [4, 768, 1024], P('chain', 'leaf')
All inputs are finite; a program needn't handle non-finite values. No bound on the sum of `pattern` on one device may be relied on, other than what follows from the above.
Results may differ from a plain program's by a relative error of at most 0.0065.
Values may be sent and summed in bfloat16 or wider, within the bound.
A program may use at most 128 MiB of HBM per device.

v0:
```python
import jax
import jax.numpy as jnp
from jax import lax
from jax.sharding import PartitionSpec as P

ROWBLK = 128


def broadcast(value, axis, root):
    mine = lax.axis_index(axis) == root
    return lax.psum(jnp.where(mine, value, jnp.zeros_like(value)), axis)


def from_partner(value, axis, stride):
    mask = 2**stride
    pairs = [(source, source ^ mask) for source in range(lax.axis_size(axis))]
    return lax.ppermute(value, axis, pairs)


def local(
    right_side, lower_rows, block_inverse, ancestor_cols, pattern, ancestor_side, ancestor_inverse
):
    rhs_rows = right_side[0]
    lower = lower_rows[0]
    inverse = block_inverse[0]
    flags = pattern[0]
    block_rows = lower.shape[0]
    chain_count = lax.axis_size("chain")
    position = lax.axis_index("chain")
    owned_rows = ancestor_side.shape[0]
    row_flags = jnp.repeat(flags.astype(jnp.float32), ROWBLK)
    pending = jnp.zeros(rhs_rows.shape, jnp.float32)
    solved = jnp.zeros(rhs_rows.shape, jnp.float32)
    arrivals = []
    for chain_step in range(chain_count):
        current = pending
        candidate = lax.cond(
            position == chain_step,
            lambda: jnp.dot(
                inverse,
                (rhs_rows - current).astype(jnp.bfloat16),
                preferred_element_type=jnp.float32,
            ),
            lambda: jnp.zeros(rhs_rows.shape, jnp.float32),
        )
        solved = solved + candidate
        arrived = broadcast(candidate.astype(jnp.bfloat16), "chain", chain_step)
        arrivals.append(arrived)
        if chain_step + 1 < chain_count:
            column_block = lower[:, chain_step * block_rows : (chain_step + 1) * block_rows]
            pending = lax.cond(
                position > chain_step,
                lambda: current
                + jnp.dot(column_block, arrived, preferred_element_type=jnp.float32),
                lambda: current,
            )
    solved_low = solved.astype(jnp.bfloat16)
    columns = ancestor_cols[0]
    product = jnp.dot(columns, solved_low, preferred_element_type=jnp.float32)
    partial_value = lax.psum_scatter(
        product * row_flags[:, None], "chain", scatter_dimension=0, tiled=True
    )
    levels = lax.axis_size("leaf").bit_length() - 1
    for level in range(levels):
        partial_value = partial_value + from_partner(partial_value, "leaf", level)
    share_rows = owned_rows // lax.axis_size("leaf")
    leaf_position = lax.axis_index("leaf")
    inverse_share = lax.dynamic_slice_in_dim(
        ancestor_inverse, leaf_position * share_rows, share_rows, 0
    )
    ancestor_solution = jnp.dot(
        inverse_share,
        (ancestor_side - partial_value).astype(jnp.bfloat16),
        preferred_element_type=jnp.float32,
    )
    return (solved[None], ancestor_solution[None])


def solution(mesh):
    return jax.shard_map(
        local,
        mesh=mesh,
        in_specs=(
            P("leaf", "chain", None),
            P("leaf", "chain", None),
            P("leaf", "chain", None),
            P("leaf", None, "chain"),
            P("leaf", None),
            P("chain", None),
            P("chain", None),
        ),
        out_specs=(P("leaf", "chain", None), P("chain", "leaf", None)),
        check_vma=False,
    )
```

profile of v0, /device:TPU:0, one launch (start us, length us, event | category | flops | bytes accessed | tf_op | source)
XLA Modules:
  0.0 701.0 jit_solution(8203343773028368888)
XLA Ops:
  7.2 7.3 %conditional.7 = (f32[1024,1024]{1,0:T(8,128)}, bf16[1024,1024]{1,0:T(8,128)(2,1)S(1)}) conditional(s32[]{:T(128)} %convert_element_type.63, () %tuple.62, (f32[1024,1024]{1,0:T(8,128)}, bf16[1024,1024]{1,0:T(8,128)(2,1)}) %tuple.117), branch_computations={%region_0.0_spmd, %region_1.0_spmd} | conditional | flops 2149580800 | bytes 12582928 | solution.py:37
  7.3 7.2 %fusion.20 = (bf16[1024,1024]{1,0:T(8,128)(2,1)S(1)}, f32[1024,1024]{1,0:T(8,128)}) fusion(bf16[1024,1024]{1,0:T(8,128)(2,1)} %get-tuple-element.59, f32[1024,1024]{1,0:T(8,128)} %get-tuple-element.60), kind=kOutput, calls=%fused_computation.30 | convolution fusion | flops 2149580800 | bytes 12582912 | tf_op jit(solution)/shard_map/cond/branch_1_fun/dot_general | solution.py:39
  16.0 58.1 %all-reduce.4.cloned.1.call-done = bf16[1024,1024]{1,0:T(8,128)(2,1)} async-done(((bf16[1024,1024]{1,0:T(8,128)(2,1)}), bf16[1024,1024]{1,0:T(8,128)(2,1)}) %all-reduce.4.cloned.1.call-update) | async-done | bytes 2097168 | tf_op jit(solution)/shard_map/psum | solution.py:11
  74.1 2.6 conditional.8
  74.1 2.5 broadcast.24
  76.6 2.8 conditional.9
  76.6 2.5 broadcast.25.clone
  79.4 1.4 broadcast_select_fusion.1
  80.9 76.0 %all-reduce.6.cloned.1.call-done = bf16[1024,1024]{1,0:T(8,128)(2,1)} async-done(((bf16[1024,1024]{1,0:T(8,128)(2,1)}), bf16[1024,1024]{1,0:T(8,128)(2,1)}) %all-reduce.6.cloned.1.call-update) | async-done | bytes 2097168 | tf_op jit(solution)/shard_map/psum | solution.py:11
  156.9 2.9 conditional.11
  156.9 2.5 broadcast.27.clone
  161.4 80.8 %all-reduce.8.cloned.1.call-done = bf16[1024,1024]{1,0:T(8,128)(2,1)} async-done(((bf16[1024,1024]{1,0:T(8,128)(2,1)}), bf16[1024,1024]{1,0:T(8,128)(2,1)}) %all-reduce.8.cloned.1.call-update) | async-done | bytes 2097168 | tf_op jit(solution)/shard_map/psum | solution.py:11
  242.3 1.6 copy-done.2
  243.8 2.5 conditional.13
  243.8 2.5 broadcast.29.clone
  246.3 7.9 %add_add_fusion = f32[1024,1024]{1,0:T(8,128)S(1)} fusion(f32[1024,1024]{1,0:T(8,128)} %get-tuple-element.98, f32[1024,1024]{1,0:T(8,128)} %get-tuple-element.96, f32[1024,1024]{1,0:T(8,128)} %get-tuple-element.86, f32[1024,1024]{1,0:T(8,128)} %get-tuple-element.94), kind=kLoop, calls=%fused_computation.18 | loop fusion | flops 3145728 | bytes 20971520 | tf_op jit(solution)/shard_map/add | solution.py:46
  254.2 2.0 copy-done.1
  256.2 12.4 %multiply_bitcast_fusion = f32[3072,1024]{0,1:T(8,128)} fusion(bf16[1,3072,1024]{2,1,0:T(8,128)(2,1)} %param.24, f32[3072]{0:T(1024)S(1)} %broadcast_bitcast_fusion, f32[1024,1024]{1,0:T(8,128)S(1)} %add_add_fusion), kind=kOutput, calls=%fused_computation.16 | convolution fusion | flops 6446645248 | bytes 23080960 | tf_op jit(solution)/shard_map/dot_general | solution.py:59
  268.6 130.9 %reduce-scatter.2.cloned.1.call-done = f32[768,1024]{0,1:T(8,128)} async-done(((f32[3072,1024]{0,1:T(8,128)}), f32[768,1024]{0,1:T(8,128)}) %reduce-scatter.2.cloned.1.call-update) | async-done | bytes 3145744 | tf_op jit(solution)/shard_map/reduce_scatter | solution.py:60
  399.5 5.9 collective-permute-done
  405.4 2.3 add.45
  407.6 1.6 collective-permute-start.1
  409.2 68.7 %collective-permute-done.1 = f32[768,1024]{0,1:T(8,128)S(1)} collective-permute-done((f32[768,1024]{0,1:T(8,128)S(1)}, f32[768,1024]{0,1:T(8,128)S(1)}, u32[]{:S(2)}, u32[]{:S(2)}) %collective-permute-start.1) | collective-permute-done | bytes 3145760 | tf_op jit(solution)/shard_map/ppermute | solution.py:17
  478.2 3.1 collective-permute-start.2
  481.3 67.8 %collective-permute-done.2 = f32[768,1024]{0,1:T(8,128)S(1)} collective-permute-done((f32[768,1024]{0,1:T(8,128)S(1)}, f32[768,1024]{0,1:T(8,128)S(1)}, u32[]{:S(2)}, u32[]{:S(2)}) %collective-permute-start.2) | collective-permute-done | bytes 3145760 | tf_op jit(solution)/shard_map/ppermute | solution.py:17
  549.5 1.5 collective-permute-start.3
  551.1 67.0 %collective-permute-done.3 = f32[768,1024]{0,1:T(8,128)S(1)} collective-permute-done((f32[768,1024]{0,1:T(8,128)S(1)}, f32[768,1024]{0,1:T(8,128)S(1)}, u32[]{:S(2)}, u32[]{:S(2)}) %collective-permute-start.3) | collective-permute-done | bytes 3145760 | tf_op jit(solution)/shard_map/ppermute | solution.py:17
  618.0 2.1 add.48
  620.1 3.0 collective-permute-start.4
  623.1 3.5 copy.14
  626.6 62.9 %collective-permute-done.4 = f32[768,1024]{0,1:T(8,128)} collective-permute-done((f32[768,1024]{0,1:T(8,128)}, f32[768,1024]{0,1:T(8,128)}, u32[]{:S(2)}, u32[]{:S(2)}) %collective-permute-start.4) | collective-permute-done | bytes 3145760 | tf_op jit(solution)/shard_map/ppermute | solution.py:17
  689.5 4.9 fusion.17
  (25 shorter events, 4.5 us)
Async XLA Ops:
  7.2 682.3 %copy-start = (bf16[768,768]{1,0:T(8,128)(2,1)S(1)}, bf16[768,768]{1,0:T(8,128)(2,1)}, u32[]{:S(2)}) copy-start(bf16[768,768]{1,0:T(8,128)(2,1)} %param.27) | copy-start | bytes 3538948
  7.2 66.9 %all-reduce.4.cloned.1.call-start = ((), (), s32[]{:S(2)}) async-start(), calls=%async_computation.1 | async-start | bytes 4194304 | tf_op jit(solution)/shard_map/psum | solution.py:11
  16.0 140.9 %all-reduce.6.cloned.1.call-start = ((), (), s32[]{:S(2)}) async-start(), calls=%async_computation.2 | async-start | bytes 4194304 | tf_op jit(solution)/shard_map/psum | solution.py:11
  80.9 161.4 %all-reduce.8.cloned.1.call-start = ((), (), s32[]{:S(2)}) async-start(), calls=%async_computation.3 | async-start | bytes 4194304 | tf_op jit(solution)/shard_map/psum | solution.py:11
  159.8 1.5 copy-start.3
  161.3 238.2 %reduce-scatter.2.cloned.1.call-start = ((), (), s32[]{:S(2)}) async-start(), calls=%async_computation.4 | async-start | bytes 15728640 | tf_op jit(solution)/shard_map/reduce_scatter | solution.py:60
  242.3 1.6 copy-start.2
  254.2 2.0 copy-start.1
  399.5 5.9 collective-permute-start
  407.6 70.2 %collective-permute-start.1 = (f32[768,1024]{0,1:T(8,128)S(1)}, f32[768,1024]{0,1:T(8,128)S(1)}, u32[]{:S(2)}, u32[]{:S(2)}) collective-permute-start(f32[768,1024]{0,1:T(8,128)S(1)} %add.45), channel_id=1, source_target_pairs={{0,8},{4,12},{8,0},{12,4},{16,24},{20,28},{24,16},{28,20},{32,40},... | collective-permute-start | bytes 9437192 | tf_op jit(solution)/shard_map/ppermute | solution.py:17
  478.2 70.9 %collective-permute-start.2 = (f32[768,1024]{0,1:T(8,128)S(1)}, f32[768,1024]{0,1:T(8,128)S(1)}, u32[]{:S(2)}, u32[]{:S(2)}) collective-permute-start(f32[768,1024]{0,1:T(8,128)S(1)} %add.46), channel_id=1, source_target_pairs={{0,16},{4,20},{8,24},{12,28},{16,0},{20,4},{24,8},{28,12},{32,48},... | collective-permute-start | bytes 9437192 | tf_op jit(solution)/shard_map/ppermute | solution.py:17
  549.5 68.5 %collective-permute-start.3 = (f32[768,1024]{0,1:T(8,128)S(1)}, f32[768,1024]{0,1:T(8,128)S(1)}, u32[]{:S(2)}, u32[]{:S(2)}) collective-permute-start(f32[768,1024]{0,1:T(8,128)S(1)} %add.47), channel_id=1, source_target_pairs={{0,32},{4,36},{8,40},{12,44},{16,48},{20,52},{24,56},{28,60},{32,0... | collective-permute-start | bytes 9437192 | tf_op jit(solution)/shard_map/ppermute | solution.py:17
  620.1 69.4 %collective-permute-start.4 = (f32[768,1024]{0,1:T(8,128)}, f32[768,1024]{0,1:T(8,128)}, u32[]{:S(2)}, u32[]{:S(2)}) collective-permute-start(f32[768,1024]{0,1:T(8,128)} %add.48), channel_id=1, source_target_pairs={{0,64},{4,68},{8,72},{12,76},{16,80},{20,84},{24,88},{28,92},{32,9... | collective-permute-start | bytes 9437192 | tf_op jit(solution)/shard_map/ppermute | solution.py:17
Sparse Core Ops, SparseCore 0:
  16.1 57.9 all-reduce.3
  81.0 75.8 all-reduce.5
  161.4 80.8 all-reduce.7
  268.7 130.7 reduce-scatter.1
where the time goes:
time: 701 us
  waiting for transfers between devices  618 us (88%)
  matrix products  24.6 us (4%)
  local copies, waits for them, and re-layouts  17.7 us (3%)
  other arithmetic  17.3 us (2%)
  between operations  13.9 us (2%)
  starting transfers between devices  9.34 us (1%)
    ppermute x5, waiting for transfers between devices, from_partner(): return lax.ppermute(value, axis, pairs)  272 us
    psum x3, waiting for transfers between devices, broadcast(): return lax.psum(jnp.where(mine, value, jnp.zeros_like(value)), axis)  215 us
    reduce_scatter x1, waiting for transfers between devices, local(): lax.psum_scatter(product * row_flags[:, None], 'chain', scatter_dimension...  131 us
  transfers between devices with their start and end apart: 9, of which 9 were waited for; matrix products, arithmetic and copies ran while one was open for 1% of the time, Pallas kernels for 0%

commit v1 on v0

--- a/solution.py
+++ b/solution.py
@@ -8,7 +8,7 @@
 
 def broadcast(value, axis, root):
     mine = lax.axis_index(axis) == root
-    return lax.psum(jnp.where(mine, value, jnp.zeros_like(value)), axis)
+    return jnp.sum(lax.all_gather(jnp.where(mine, value, jnp.zeros_like(value)), axis), axis=0)
 
 
 def from_partner(value, axis, stride):

time: 701 us -> 853 us (1.22)
  waiting for transfers between devices: 618 us -> 766 us
    all_gather x0 -> x3, waiting for transfers between devices: none -> 334 us  [broadcast(): lax.all_gather(jnp.where(mine, value, jnp.zeros_like(value)), axis)]
    psum x3 -> x0, waiting for transfers between devices: 215 us -> none  [broadcast(): return lax.psum(jnp.where(mine, value, jnp.zeros_like(value)), axis)]
    reduce_scatter x1, waiting for transfers between devices: 131 us -> 159 us  [local(): lax.psum_scatter(product * row_flags[:, None], 'chain', scatter_dimension...]
  transfers between devices with their start and end apart: 9 -> 9, of which waited for: 9 -> 9; matrix products, arithmetic and copies ran while one was open for 1% -> 0% of each run, Pallas kernels for 0% -> 0%
where the time goes in v1:
time: 853 us; the launch traced here: 851 us
  waiting for transfers between devices  766 us (90%)
  matrix products  25.3 us (3%)
  local copies, waits for them, and re-layouts  19 us (2%)
  other arithmetic  17.6 us (2%)
  between operations  13.9 us (2%)
  starting transfers between devices  9.34 us (1%)
    all_gather x3, waiting for transfers between devices, broadcast(): lax.all_gather(jnp.where(mine, value, jnp.zeros_like(value)), axis)  334 us
    ppermute x5, waiting for transfers between devices, from_partner(): return lax.ppermute(value, axis, pairs)  272 us
    reduce_scatter x1, waiting for transfers between devices, local(): lax.psum_scatter(product * row_flags[:, None], 'chain', scatter_dimension...  159 us
  transfers between devices with their start and end apart: 9, of which 9 were waited for; matrix products, arithmetic and copies ran while one was open for 0% of the time, Pallas kernels for 0%

profile of v1, /device:TPU:0, one launch (start us, length us, event | category | flops | bytes accessed | tf_op | source)
XLA Modules:
  0.0 850.8 jit_solution(11306244337109551330)
XLA Ops:
  7.2 10.8 %conditional.7 = (f32[1024,1024]{1,0:T(8,128)}, bf16[1024,1024]{0,1:T(8,128)(2,1)S(1)}) conditional(s32[]{:T(128)} %convert_element_type.69, () %tuple.62, (f32[1024,1024]{1,0:T(8,128)}, bf16[1024,1024]{1,0:T(8,128)(2,1)}) %tuple.118), branch_computations={%region_0.0_spmd, %region_1.0_spmd} | conditional | flops 2149580800 | bytes 16777232 | solution.py:37
  7.3 7.9 fusion.20
  15.2 2.9 copy.26
  18.1 1.5 broadcast_select_fusion.2
  19.7 82.4 %all-gather.7.cloned.1.call-done = bf16[4096,1024]{0,1:T(8,128)(2,1)} async-done(((bf16[1024,1024]{0,1:T(8,128)(2,1)}), bf16[4096,1024]{0,1:T(8,128)(2,1)}) %all-gather.7.cloned.1.call-update) | async-done | bytes 8388624 | tf_op jit(solution)/shard_map/all_gather | solution.py:11
  102.1 2.5 conditional.8
  102.1 2.5 broadcast.24
  104.6 2.8 conditional.9
  104.6 2.5 broadcast.25.clone
  109.0 123.5 %all-gather.9.cloned.1.call-done = bf16[4096,1024]{0,1:T(8,128)(2,1)} async-done(((bf16[1024,1024]{0,1:T(8,128)(2,1)}), bf16[4096,1024]{0,1:T(8,128)(2,1)}) %all-gather.9.cloned.1.call-update) | async-done | bytes 8388624 | tf_op jit(solution)/shard_map/all_gather | solution.py:11
  232.5 2.8 conditional.11
  232.5 2.5 broadcast.27.clone
  237.0 128.4 %all-gather.11.cloned.1.call-done = bf16[4096,1024]{0,1:T(8,128)(2,1)} async-done(((bf16[1024,1024]{0,1:T(8,128)(2,1)}), bf16[4096,1024]{0,1:T(8,128)(2,1)}) %all-gather.11.cloned.1.call-update) | async-done | bytes 8388624 | tf_op jit(solution)/shard_map/all_gather | solution.py:11
  365.4 2.5 conditional.13
  365.4 2.5 broadcast.29.clone
  367.9 7.9 add_add_fusion
  375.8 2.0 copy-done.1
  377.8 12.4 %multiply_bitcast_fusion = f32[3072,1024]{0,1:T(8,128)} fusion(bf16[1,3072,1024]{2,1,0:T(8,128)(2,1)} %param.24, f32[3072]{0:T(1024)S(1)} %broadcast_bitcast_fusion, f32[1024,1024]{1,0:T(8,128)S(1)} %add_add_fusion), kind=kOutput, calls=%fused_computation.16 | convolution fusion | flops 6446645248 | bytes 23080960 | tf_op jit(solution)/shard_map/dot_general | solution.py:59
  390.2 159.1 %reduce-scatter.2.cloned.1.call-done = f32[768,1024]{0,1:T(8,128)} async-done(((f32[3072,1024]{0,1:T(8,128)}), f32[768,1024]{0,1:T(8,128)}) %reduce-scatter.2.cloned.1.call-update) | async-done | bytes 3145744 | tf_op jit(solution)/shard_map/reduce_scatter | solution.py:60
  549.3 5.9 collective-permute-done
  555.2 2.3 add.39
  557.5 1.6 collective-permute-start.1
  559.0 68.7 %collective-permute-done.1 = f32[768,1024]{0,1:T(8,128)S(1)} collective-permute-done((f32[768,1024]{0,1:T(8,128)S(1)}, f32[768,1024]{0,1:T(8,128)S(1)}, u32[]{:S(2)}, u32[]{:S(2)}) %collective-permute-start.1) | collective-permute-done | bytes 3145760 | tf_op jit(solution)/shard_map/ppermute | solution.py:17
  628.1 3.1 collective-permute-start.2
  631.2 67.8 %collective-permute-done.2 = f32[768,1024]{0,1:T(8,128)S(1)} collective-permute-done((f32[768,1024]{0,1:T(8,128)S(1)}, f32[768,1024]{0,1:T(8,128)S(1)}, u32[]{:S(2)}, u32[]{:S(2)}) %collective-permute-start.2) | collective-permute-done | bytes 3145760 | tf_op jit(solution)/shard_map/ppermute | solution.py:17
  699.3 1.5 collective-permute-start.3
  700.9 67.0 %collective-permute-done.3 = f32[768,1024]{0,1:T(8,128)S(1)} collective-permute-done((f32[768,1024]{0,1:T(8,128)S(1)}, f32[768,1024]{0,1:T(8,128)S(1)}, u32[]{:S(2)}, u32[]{:S(2)}) %collective-permute-start.3) | collective-permute-done | bytes 3145760 | tf_op jit(solution)/shard_map/ppermute | solution.py:17
  767.9 2.1 add.42
  769.9 3.0 collective-permute-start.4
  772.9 3.5 copy.21
  776.4 62.9 %collective-permute-done.4 = f32[768,1024]{0,1:T(8,128)} collective-permute-done((f32[768,1024]{0,1:T(8,128)}, f32[768,1024]{0,1:T(8,128)}, u32[]{:S(2)}, u32[]{:S(2)}) %collective-permute-start.4) | collective-permute-done | bytes 3145760 | tf_op jit(solution)/shard_map/ppermute | solution.py:17
  839.3 4.9 fusion.17
  (24 shorter events, 4.7 us)
Async XLA Ops:
  7.2 832.1 %copy-start = (bf16[768,768]{1,0:T(8,128)(2,1)S(1)}, bf16[768,768]{1,0:T(8,128)(2,1)}, u32[]{:S(2)}) copy-start(bf16[768,768]{1,0:T(8,128)(2,1)} %param.27) | copy-start | bytes 3538948
  7.2 94.9 %all-gather.7.cloned.1.call-start = ((), (), s32[]{:S(2)}) async-start(), calls=%async_computation.2 | async-start | bytes 10485760 | tf_op jit(solution)/shard_map/all_gather | solution.py:11
  19.6 212.9 %all-gather.9.cloned.1.call-start = ((), (), s32[]{:S(2)}) async-start(), calls=%async_computation.3 | async-start | bytes 10485760 | tf_op jit(solution)/shard_map/all_gather | solution.py:11
  108.9 256.4 %all-gather.11.cloned.1.call-start = ((), (), s32[]{:S(2)}) async-start(), calls=%async_computation.4 | async-start | bytes 10485760 | tf_op jit(solution)/shard_map/all_gather | solution.py:11
  235.3 1.6 copy-start.2
  236.9 312.5 %reduce-scatter.2.cloned.1.call-start = ((), (), s32[]{:S(2)}) async-start(), calls=%async_computation.1 | async-start | bytes 15728640 | tf_op jit(solution)/shard_map/reduce_scatter | solution.py:60
  375.8 2.0 copy-start.1
  549.3 5.9 collective-permute-start
  557.5 70.2 %collective-permute-start.1 = (f32[768,1024]{0,1:T(8,128)S(1)}, f32[768,1024]{0,1:T(8,128)S(1)}, u32[]{:S(2)}, u32[]{:S(2)}) collective-permute-start(f32[768,1024]{0,1:T(8,128)S(1)} %add.39), channel_id=1, source_target_pairs={{0,8},{4,12},{8,0},{12,4},{16,24},{20,28},{24,16},{28,20},{32,40},... | collective-permute-start | bytes 9437192 | tf_op jit(solution)/shard_map/ppermute | solution.py:17
  628.1 70.9 %collective-permute-start.2 = (f32[768,1024]{0,1:T(8,128)S(1)}, f32[768,1024]{0,1:T(8,128)S(1)}, u32[]{:S(2)}, u32[]{:S(2)}) collective-permute-start(f32[768,1024]{0,1:T(8,128)S(1)} %add.40), channel_id=1, source_target_pairs={{0,16},{4,20},{8,24},{12,28},{16,0},{20,4},{24,8},{28,12},{32,48},... | collective-permute-start | bytes 9437192 | tf_op jit(solution)/shard_map/ppermute | solution.py:17
  699.3 68.5 %collective-permute-start.3 = (f32[768,1024]{0,1:T(8,128)S(1)}, f32[768,1024]{0,1:T(8,128)S(1)}, u32[]{:S(2)}, u32[]{:S(2)}) collective-permute-start(f32[768,1024]{0,1:T(8,128)S(1)} %add.41), channel_id=1, source_target_pairs={{0,32},{4,36},{8,40},{12,44},{16,48},{20,52},{24,56},{28,60},{32,0... | collective-permute-start | bytes 9437192 | tf_op jit(solution)/shard_map/ppermute | solution.py:17
  769.9 69.4 %collective-permute-start.4 = (f32[768,1024]{0,1:T(8,128)}, f32[768,1024]{0,1:T(8,128)}, u32[]{:S(2)}, u32[]{:S(2)}) collective-permute-start(f32[768,1024]{0,1:T(8,128)} %add.42), channel_id=1, source_target_pairs={{0,64},{4,68},{8,72},{12,76},{16,80},{20,84},{24,88},{28,92},{32,9... | collective-permute-start | bytes 9437192 | tf_op jit(solution)/shard_map/ppermute | solution.py:17
Sparse Core Ops, SparseCore 0:
  19.7 82.2 all-gather.6
  109.1 123.3 all-gather.8
  237.0 128.3 all-gather.10
  390.3 158.9 reduce-scatter.1
